TPU v7x, 32 devices: a whole 2x2x4 slice. The times are simulated.
32 devices in a mesh: gx: 4 (over y, x), gy: 8 (over z, core).
Axes of the slice: x: 2, y: 2, z: 4, core: 2. Of those that a mesh axis runs over, the one named last changes fastest.
Arguments:
- atom_cell: int32 [4, 8, 4096], P('gx', 'gy'), may hold values from 0 to 49151
- atom_frac: float32 [3, 4, 8, 4096], P(None, 'gx', 'gy'), may hold values from 0 to 1
- atom_charge: float32 [4, 8, 4096], P('gx', 'gy'), may hold values from -6 to 6
- atom_count: int32 [4, 8], P('gx', 'gy'), may hold values from 1024 to 4096, as said below
- fine_kernel: float32 [9, 9, 9], replicated, may hold values from -1.8 to 1.8
- middle_kernel: float32 [9, 9, 9], replicated, may hold values from -0.9 to 0.9
- coarse_kernel: float32 [9, 9, 9], replicated, may hold values from -0.36 to 0.36
Outputs:
- potential: float32 [64, 192, 128], P('gx', 'gy')
- forces: float32 [3, 4, 8, 4096], P(None, 'gx', 'gy')
Inputs may be any that keep to these rules, and one draw needn't show every extreme that they name: `atom_count`: slots at or past a block's count hold no atom. At least one block is full in every draw; about a quarter of the blocks are nearly full and the rest hold a quarter to a half of 4096.
All inputs are finite; a program needn't handle non-finite values.
Results may differ from a plain program's by a relative error of at most 0.0003.
Values sent between devices are 32-bit elements; how exact they have to be, the bound alone decides.
A program may use at most 128 MiB of HBM per device.

v0:
```python
import jax
import jax.numpy as jnp
import ml_dtypes
import numpy as np
from jax import lax
from jax.experimental import pallas as pl
from jax.experimental.pallas import tpu as pltpu
from jax.sharding import PartitionSpec as P

CX = 16
CY = 24
NZ = 128
KERNEL = 9
HALF = KERNEL // 2
REACH = HALF + 1
LANES = 128
LAYERS = CX + 1
TOP_ROWS = -(-LAYERS * (CY + 1) // 16) * 16
FORCE_CHUNK = 256
SPREAD_PART = 512
FORCE_UNROLL = 8
LEVELS = 3
MESH = pl.DeviceIdType.MESH

BX = tuple(CX >> k for k in range(LEVELS))
BY = tuple(CY >> k for k in range(LEVELS))
ZS = tuple(NZ >> k for k in range(LEVELS))
PAIR = tuple((size + 2) // 2 for size in BX)
PERIOD = tuple(-(-(size + 1 + 2 * HALF) // 8) * 8 for size in BY)
WINDOW = (CX + 1, *(size + 1 + 2 * HALF for size in BX[1:]))
SPECTRA = tuple(size + 2 * HALF for size in PAIR)
ROWS = (32, 16, 8)
FIRST_LANE = (0, 0, ZS[1])
GRID_ROWS = (CX + 2) * CY
LOW_ROWS = ((BX[1] + 1) * ROWS[1], (BX[2] + 1) * ROWS[2])


def strip_row(x):
    return x if x < 12 else x + 4


def np_hat(distance):
    return np.maximum(1.0 - np.abs(distance), 0.0)


def np_ring_hat(distance, period):
    distance = np.abs(distance)
    return np.maximum(1.0 - np.minimum(distance, period - distance), 0.0)


def np_split(value):
    high = value.astype(np.float32).astype(ml_dtypes.bfloat16)
    low = (value - high.astype(np.float64)).astype(ml_dtypes.bfloat16)
    return high, low


def fine_places():
    xs, ys = np.full(GRID_ROWS, -1e6), np.full(GRID_ROWS, -1e6)
    for x in range(CX + 1):
        for y in range(CY):
            xs[x * CY + y], ys[x * CY + y] = x, y
        xs[(CX + 1) * CY + strip_row(x)], ys[(CX + 1) * CY + strip_row(x)] = x, CY
    return xs, ys


def transfer_xy():
    xs, ys = fine_places()
    parts = []
    for level in (1, 2):
        scale = 0.5**level
        layers = np.repeat(np.arange(BX[level] + 1), ROWS[level])
        rows = np.tile(np.arange(ROWS[level]), BX[level] + 1)
        weight = np_hat(xs[:, None] * scale - layers[None, :]) * np_hat(ys[:, None] * scale - rows[None, :])
        parts.append(weight * (rows <= BY[level])[None, :])
    return np.concatenate(parts, axis=1)


def transfer_z():
    weight = np.zeros((NZ, LANES))
    for level in (1, 2):
        z, low = np.arange(NZ)[:, None], np.arange(ZS[level])[None, :]
        weight[:, FIRST_LANE[level] : FIRST_LANE[level] + ZS[level]] = np_ring_hat(z * 0.5**level - low, ZS[level])
    return weight


def z_forward(level):
    size = ZS[level]
    angle = 2 * np.pi * np.arange(size)[:, None] * np.arange(size)[None, :] / size
    c, s = np.cos(angle), np.sin(angle)
    table = np.zeros((LANES, 2 * LANES))
    first = FIRST_LANE[level]
    if level == 0:
        table[:, :LANES], table[:, LANES:] = c, -s
    else:
        rows = slice(first, first + size)
        table[rows, :size], table[rows, size : 2 * size] = c, -s
        table[rows, LANES : LANES + size], table[rows, LANES + size : LANES + 2 * size] = -s, -c
    high, low = np_split(table)
    return np.concatenate([high, high, low], axis=0)


def z_inverse(level):
    size = ZS[level]
    angle = 2 * np.pi * np.arange(size)[:, None] * np.arange(size)[None, :] / size
    raised = np_ring_hat(np.arange(NZ)[None, :] * 0.5**level - np.arange(size)[:, None], size)
    c, s = np.cos(angle) @ raised / size, np.sin(angle) @ raised / size
    table = np.concatenate([np.concatenate([c, s], axis=1), np.concatenate([-s, c], axis=1)], axis=0)
    rows = 2 * LANES if level == 0 else LANES
    table = np.concatenate([table, np.zeros((rows - table.shape[0], 2 * LANES))], axis=0)
    high, low = np_split(table)
    return np.concatenate([high, high, low], axis=0)


def y_forward(level):
    size = PERIOD[level]
    angle = 2 * np.pi * np.arange(size)[:, None] * np.arange(size)[None, :] / size
    c, s = np.cos(angle), np.sin(angle)
    high, low = np_split(np.block([[c, s], [-s, c]]))
    return np.concatenate([high, high, low], axis=1)


def y_inverse(level):
    size = PERIOD[level]
    angle = 2 * np.pi * np.arange(ROWS[level])[:, None] * np.arange(size)[None, :] / size
    keep = (np.arange(ROWS[level]) <= BY[level])[:, None]
    c, s = np.cos(angle) * keep / size, np.sin(angle) * keep / size
    table = np.block([[c, -s], [s, c]]) if level == 0 else np.block([[c, -s]])
    if table.shape[0] < 16:
        table = np.concatenate([table, np.zeros((16 - table.shape[0], 2 * size))], axis=0)
    high, low = np_split(table)
    return np.concatenate([high, high, low], axis=1)


def stack_split(table, axis):
    high, low = np_split(table)
    return np.concatenate([high, high, low], axis=axis)


def taps_z(level):
    size = ZS[level]
    angle = 2 * np.pi * (np.arange(KERNEL) - HALF)[:, None] * np.arange(size)[None, :] / size
    table = np.zeros((LANES, 2 * LANES))
    for copy in range(1 if level == 0 else 2):
        table[:KERNEL, copy * size : (copy + 1) * size] = np.cos(angle)
        table[:KERNEL, LANES + copy * size : LANES + (copy + 1) * size] = np.sin(angle)
    return stack_split(table, 0)


def taps_y(level):
    size = PERIOD[level]
    angle = 2 * np.pi * np.arange(size)[:, None] * (np.arange(16) - HALF)[None, :] / size
    keep = (np.arange(16) < KERNEL)[None, :]
    c, s = np.cos(angle) * keep, np.sin(angle) * keep
    return stack_split(np.block([[c, -s], [s, c]]), 1)


def tables():
    xy = transfer_xy()
    z = transfer_z()
    bf16 = ml_dtypes.bfloat16
    stacked = [xy.astype(bf16)]
    for level in range(LEVELS):
        stacked += [z_forward(level), z_inverse(level), y_forward(level), y_inverse(level), taps_z(level), taps_y(level)]
    places, first = [], 0
    for table in stacked:
        places.append((slice(first, first + table.shape[0]), slice(0, table.shape[1])))
        first += table.shape[0]
    whole = np.zeros((first, 2 * LANES), bf16)
    for place, table in zip(places, stacked):
        whole[place] = table
    return [xy.T.astype(bf16), np.concatenate([z, z], axis=0).astype(bf16), whole], places


class Part:
    def __init__(self, ref, place):
        self.ref, self.place = ref, place

    def __getitem__(self, _):
        return self.ref[self.place]


def split(value):
    high = value.astype(jnp.bfloat16)
    return high, (value - high.astype(jnp.float32)).astype(jnp.bfloat16)


def matmul(a, b):
    return jnp.dot(a, b, preferred_element_type=jnp.float32)


def matmul_nt(a, b):
    return lax.dot_general(a, b, (((1,), (1,)), ((), ())), preferred_element_type=jnp.float32)


def rows_iota(rows, columns):
    return lax.broadcasted_iota(jnp.int32, (rows, columns), 0)


def bases(cell):
    return cell // (CY * NZ), (cell // NZ) % CY, cell % NZ


def wide(value, dtype):
    return jnp.broadcast_to(value, (16, value.shape[1])).astype(dtype)


def row_patterns(columns):
    row = rows_iota(16, columns)
    patterns = []
    for tile in range(TOP_ROWS // 16):
        xs, ys = [], []
        for part in range(2):
            first = tile * 16 + part * 8
            if first < LAYERS * CY:
                xs.append(first // CY)
                ys.append(row + (first % CY - 8 * part))
            else:
                at = row + (first - LAYERS * CY - 8 * part)
                xs.append(jnp.where(at < LAYERS, at, -9))
                ys.append(jnp.full_like(row, CY))
        if all(isinstance(x, int) for x in xs) and xs[0] == xs[1]:
            x = jnp.full((16, columns), xs[0], jnp.int16)
        else:
            x = jnp.where(row < 8, xs[0], xs[1]).astype(jnp.int16)
        patterns.append((x, jnp.where(row < 8, ys[0], ys[1]).astype(jnp.int16)))
    return patterns


def spread_sides(count_ref, cell_ref, frac_ref, charge_ref, start, patterns, row_z):
    bf16, i16 = jnp.bfloat16, jnp.int16
    part = slice(start, start + SPREAD_PART)
    base_x, base_y, base_z = bases(cell_ref[0, :, part])
    f = [frac_ref[k, 0, :, part] for k in range(3)]
    slot = start + lax.broadcasted_iota(jnp.int32, (1, SPREAD_PART), 1)
    charge = jnp.where(slot < count_ref[...], charge_ref[0, :, part], 0.0)
    nothing = jnp.zeros((16, SPREAD_PART), bf16)
    x_at, x_next = wide(base_x, i16), wide(base_x + 1, i16)
    y_at, y_next = wide(base_y, i16), wide(base_y + 1, i16)
    corner = {}
    for a, along_x in enumerate((charge * (1.0 - f[0]), charge * f[0])):
        for b, along_y in enumerate((1.0 - f[1], f[1])):
            high, low = split(along_x * along_y)
            corner[a, b] = (wide(high, bf16), wide(low, bf16))
    highs, lows = [], []
    known = {}
    for tile, (xs, ys) in enumerate(patterns):
        key = tile % 3 if (tile + 1) * 16 <= LAYERS * CY else tile
        if key not in known:
            here, above = ys == y_at, ys == y_next
            known[key] = [
                [jnp.where(here, corner[a, 0][k], jnp.where(above, corner[a, 1][k], nothing)) for k in range(2)]
                for a in range(2)
            ]
        here, above = xs == x_at, xs == x_next
        for k, target in enumerate((highs, lows)):
            target.append(jnp.where(here, known[key][0][k], jnp.where(above, known[key][1][k], nothing)))
    weights = [[wide(piece, bf16) for piece in split(value)] for value in (1.0 - f[2], f[2])]
    sides = ([], [])
    z_at, z_next = wide(base_z, i16), wide((base_z + 1) & (NZ - 1), i16)
    for rows in row_z:
        here, above = rows == z_at, rows == z_next
        for k in range(2):
            sides[k].append(jnp.where(here, weights[0][k], jnp.where(above, weights[1][k], nothing)))
    return [jnp.concatenate(pieces, axis=0) for pieces in (highs, lows, *sides)]


def spread(count_ref, cell_ref, frac_ref, charge_ref, grid_ref):
    slots = cell_ref.shape[-1]
    patterns = row_patterns(SPREAD_PART)
    row_z = [(rows_iota(16, SPREAD_PART) + first).astype(jnp.int16) for first in range(0, NZ, 16)]
    parts = [
        spread_sides(count_ref, cell_ref, frac_ref, charge_ref, start, patterns, row_z)
        for start in range(0, slots, SPREAD_PART)
    ]
    top_high, top_low, z_high, z_low = [jnp.concatenate(pieces, axis=1) for pieces in zip(*parts)]
    both = matmul_nt(top_high, jnp.concatenate([z_high, z_low], axis=0))
    value = both[:, :LANES] + both[:, LANES:] + matmul_nt(top_low, z_high)
    layers = LAYERS * CY
    grid_ref[:LAYERS] = value[:layers].reshape(LAYERS, CY, LANES)
    grid_ref[LAYERS] = jnp.zeros((CY, LANES), jnp.float32)
    for x in range(LAYERS):
        grid_ref[LAYERS, strip_row(x) : strip_row(x) + 1, :] = value[layers + x : layers + x + 1]


def lane_iota():
    return lax.broadcasted_iota(jnp.int32, (1, 1, LANES), 2)


def restrict(grid_ref, down_ref, down_z_ref, middle_ref, low_ref):
    high, low = split(grid_ref[...].reshape(GRID_ROWS, LANES))
    both = matmul(down_ref[...], jnp.concatenate([high, low], axis=1))
    high, low = split(both[:, :LANES] + both[:, LANES:])
    value = matmul(jnp.concatenate([high, low], axis=1), down_z_ref[...])
    middle = value[: LOW_ROWS[0]].reshape(BX[1] + 1, ROWS[1], LANES)
    coarse = value[LOW_ROWS[0] :].reshape(BX[2] + 1, ROWS[2], LANES)
    twice = jnp.concatenate([coarse, coarse], axis=1)
    first = BX[1] - BX[2]
    mine = lane_iota() < FIRST_LANE[2]
    middle_ref[:first] = middle[:first]
    middle_ref[first:] = jnp.where(mine, middle[first:], twice)
    low_ref[...] = jnp.where(mine, middle[: BX[2] + 1], twice)


def build_taps(level, kernel_ref, padded_ref, z_ref, y_ref, real_ref, imag_ref):
    padded_ref[...] = jnp.zeros_like(padded_ref)
    padded_ref[:, :KERNEL, :KERNEL] = kernel_ref[...]
    along_z = matmul(three(padded_ref[...].reshape(KERNEL * 16, LANES), 1), z_ref[...])
    size = PERIOD[level]
    for shift in range(0, KERNEL, 2):
        pieces = []
        for one in range(shift, min(shift + 2, KERNEL)):
            rows = along_z[one * 16 : (one + 1) * 16]
            pieces.append(three(jnp.concatenate([rows[:, :LANES], rows[:, LANES:]], axis=0), 0))
        both = matmul(y_ref[...], jnp.concatenate(pieces, axis=1))
        for k in range(len(pieces)):
            real_ref[shift + k] = both[:size, k * LANES : (k + 1) * LANES]
            imag_ref[shift + k] = both[size:, k * LANES : (k + 1) * LANES]


def three(value, axis):
    high, low = split(value)
    return jnp.concatenate([high, low, high], axis=axis)


def add_spectra(level, source_ref, slots, taps, tables, along_z_ref, spectrum_ref, sums_ref, fresh):
    forward_z, _, forward_y, _ = tables
    size, pair = PERIOD[level], PAIR[level]
    used = len(slots)
    flat = source_ref[...].reshape(used * size, LANES)
    half = (used // 2 + 1) * size
    for rows in (slice(0, half), slice(half, used * size)):
        along_z_ref[rows] = matmul(three(flat[rows], 1), forward_z[...])

    def part(layer, which):
        slot = slots[layer]
        return along_z_ref[slot * size : (slot + 1) * size, which * LANES : (which + 1) * LANES]

    def combined(layer):
        if layer not in slots:
            return [-part(layer + pair, 1), part(layer + pair, 0)]
        if layer + pair not in slots:
            return [part(layer, 0), part(layer, 1)]
        return [part(layer, 0) - part(layer + pair, 1), part(layer, 1) + part(layer + pair, 0)]

    present = [layer for layer in range(SPECTRA[level]) if layer in slots or layer + pair in slots]
    for first in range(0, len(present), 2):
        group = present[first : first + 2]
        pieces = [three(jnp.concatenate(combined(layer), axis=0), 0) for layer in group]
        both = matmul(forward_y[...], jnp.concatenate(pieces, axis=1))
        for k, layer in enumerate(group):
            spectrum_ref[layer] = both[:, k * LANES : (k + 1) * LANES]
    real_ref, imag_ref = taps
    for out in range(pair):
        for tile in range(0, size, 8):
            rows, rest = slice(tile, tile + 8), slice(size + tile, size + tile + 8)
            real = jnp.zeros((8, LANES), jnp.float32) if fresh else sums_ref[out, rows]
            imag = jnp.zeros((8, LANES), jnp.float32) if fresh else sums_ref[out, rest]
            for shift in range(KERNEL):
                if out + shift in present:
                    a, b = spectrum_ref[out + shift, rows], spectrum_ref[out + shift, rest]
                    c, s = real_ref[shift, rows], imag_ref[shift, rows]
                    real = real + a * c - b * s
                    imag = imag + a * s + b * c
            sums_ref[out, rows] = real
            sums_ref[out, rest] = imag


def from_spectra(level, tables, sums_ref):
    _, inverse_z, _, inverse_y = tables
    pair, rows = PAIR[level], ROWS[level]
    lines = []
    for first in range(0, pair, 2):
        group = range(first, min(first + 2, pair))
        both = matmul(inverse_y[...], jnp.concatenate([three(sums_ref[out], 0) for out in group], axis=1))
        for k in range(len(group)):
            line = both[:rows, k * LANES : (k + 1) * LANES]
            if level == 0:
                line = jnp.concatenate([line, both[rows:, k * LANES : (k + 1) * LANES]], axis=1)
            lines.append(line)
    half = pair // 2 + 1
    values = []
    for group in (lines[:half], lines[half:]):
        value = matmul(three(jnp.concatenate(group, axis=0), 1), inverse_z[...])
        values += [value[k * rows : (k + 1) * rows] for k in range(len(group))]
    layers = [value[:, :LANES] for value in values] + [value[:, LANES:] for value in values]
    return layers[: BX[level] + 1]


GRID, MIDDLE, LOW, LANDED = range(4)


def side(step, size):
    return {-1: (0, REACH), 0: (0, size + 1), 1: (size - HALF, REACH)}[step]


class Message:
    def __init__(self, kind, dx, dy, source, layers, rows, relayed=None):
        self.kind, self.dx, self.dy = kind, dx, dy
        self.source, self.layers, self.rows, self.relayed = source, layers, rows, relayed
        self.hop = (dx, dy) if relayed is None else (0, dy)
        self.local = (layers, rows)
        if relayed is not None:
            self.local = ((0, layers[1]), (rows[0] - relayed.rows[0], rows[1]))


def plan_messages():
    near, far, face, strip = {}, {}, {}, {}
    top, bottom = (CY - 8, 8), (0, 8)
    for dx, layer in ((-2, 0), (2, BX[1])):
        far[dx, 0] = Message("far", dx, 0, LOW if dx < 0 else MIDDLE, (layer, 1), (0, 8))
    for dx in (-1, 1):
        near[dx, 0] = Message("near", dx, 0, LOW if dx < 0 else MIDDLE, side(dx, BX[1]), (0, ROWS[1]))
        strip[dx, 0] = Message("strip", dx, 0, GRID, (CX + 1, 1), bottom if dx < 0 else top)
        for name, rows in (("top", top), ("bottom", bottom), ("centre", (8, CY - 16))):
            face[dx, name] = Message("face", dx, 0, GRID, side(dx, BX[0]), rows)
    for dy in (-1, 1):
        rows = bottom if dy < 0 else (ROWS[1] - 8, 8)
        near[0, dy] = Message("near", 0, dy, MIDDLE, side(0, BX[1]), rows)
        face[0, dy] = Message("face", 0, dy, GRID, side(0, BX[0]), bottom if dy < 0 else top)
        for dx in (-2, 2):
            far[dx, dy] = Message("far", dx, dy, LANDED, far[dx, 0].layers, (0, 8), far[dx, 0])
        for dx in (-1, 1):
            near[dx, dy] = Message("near", dx, dy, LANDED, near[dx, 0].layers, rows, near[dx, 0])
            first = face[dx, "bottom" if dy < 0 else "top"]
            face[dx, dy] = Message("face", dx, dy, LANDED, first.layers, first.rows, first)
    strip[0, 1] = Message("strip", 0, 1, GRID, (CX + 1, 1), (0, CY))
    for dx in (-1, 1):
        strip[dx, 1] = Message("strip", dx, 1, LANDED, (CX + 1, 1), strip[dx, 0].rows, strip[dx, 0])
    sides = (-1, 1)
    first = [near[dx, 0] for dx in sides]
    first += [face[dx, name] for name in ("top", "bottom") for dx in sides] + [strip[dx, 0] for dx in sides]
    first += [near[0, dy] for dy in sides] + [far[dx, 0] for dx in (-2, 2)]
    first += [face[0, dy] for dy in sides] + [strip[0, 1]] + [face[dx, "centre"] for dx in sides]
    second = [near[dx, dy] for dx in sides for dy in sides] + [far[dx, dy] for dx in (-2, 2) for dy in sides]
    second += [face[dx, dy] for dy in (1, -1) for dx in sides] + [strip[dx, 1] for dx in sides]
    return first, second


FIRST, SECOND = plan_messages()
PLAN = FIRST + SECOND


def add_rows(window_ref, layer, first, piece):
    rows = slice(first, first + piece.shape[-2])
    layers = slice(layer, layer + piece.shape[0])
    window_ref[layers, rows, :] = window_ref[layers, rows, :] + piece


def add_level_rows(window_ref, level, layer, dy, piece):
    size = BY[level]
    if dy == 0:
        add_rows(window_ref, layer, 0, piece[:, : size + 1])
    elif dy < 0:
        add_rows(window_ref, layer, size, piece[:, :REACH])
    else:
        base = piece.shape[-2] - 8 if piece.shape[-2] > 8 else (size // 8) * 8
        first = size - HALF - base
        add_rows(window_ref, layer, PERIOD[level] - HALF, piece[:, first : first + HALF])
        add_rows(window_ref, layer, 0, piece[:, first + HALF : first + HALF + 1])


def add_low(windows, message, landed):
    dx, dy, first = message.dx, message.dy, message.layers[0]
    if message.kind == "far":
        layer = HALF + (0 if dx < 0 else BX[2]) - dx * BX[2]
        add_level_rows(windows[2], 2, layer, dy, landed[...])
        return
    add_level_rows(windows[1], 1, HALF + first - dx * BX[1], dy, landed[...])
    ride = BX[1] - BX[2] if dx == 0 else 0
    add_level_rows(windows[2], 2, HALF - dx * BX[2], dy, landed[ride : ride + BX[2] + 1, :8, :])


def add_fine(window_ref, message, landed):
    dx, dy, rows = message.dx, message.dy, message.rows
    offset = {-1: REACH, 0: 0, 1: HALF - BX[0]}[dx]
    if message.kind == "strip":
        low, size = side(dx, BX[0])
        target = CY if dy == 0 else 0
        for k in range(size):
            place = strip_row(low + k) - rows[0]
            layer = offset + low + k
            window_ref[layer, target : target + 1, :] = (
                window_ref[layer, target : target + 1, :] + landed[0, place : place + 1, :]
            )
        return
    first, count = message.layers
    layers = slice(offset + first, offset + first + count)
    row = lax.broadcasted_iota(jnp.int32, (1, 8, LANES), 1)
    value = landed[...]
    at = slice(rows[0], rows[0] + rows[1])
    if dy < 0:
        at, value = slice(CY, CY + 8), jnp.where(row < REACH, value, 0.0)
    elif dy > 0:
        at, value = slice(PERIOD[0] - 8, PERIOD[0]), jnp.where(row >= 8 - HALF, value, 0.0)
    window_ref[layers, at, :] = window_ref[layers, at, :] + value


def grid_kernel(sizes, n_tables, places, *refs):
    count_ref, cell_ref, frac_ref, charge_ref = refs[:4]
    kernels = refs[4:7]
    table_sources = refs[7 : 7 + n_tables]
    out_ref = refs[7 + n_tables]
    scratch = list(refs[8 + n_tables :])

    def take(count):
        taken = scratch[:count]
        del scratch[:count]
        return taken

    grid_ref, middle_ref, low_ref, padded_ref = take(4)
    table_refs = take(n_tables)
    windows, reals, imags, along_z, spectra, sums = take(3), take(3), take(3), take(3), take(3), take(3)
    (edges_ref,) = take(1)
    landed = take(len(PLAN))
    send_sem, recv_sem, table_sem = take(3)

    me = (lax.axis_index("gx"), lax.axis_index("gy"))

    def device(dx, dy):
        return (lax.rem(me[0] + dx + sizes[0], sizes[0]), lax.rem(me[1] + dy + sizes[1], sizes[1]))

    barrier = pltpu.get_barrier_semaphore()
    around = sorted({message.hop for message in PLAN})
    for dx, dy in around:
        pl.semaphore_signal(barrier, inc=1, device_id=device(dx, dy), device_id_type=MESH)
    loads = [
        pltpu.make_async_copy(source, target, table_sem.at[index])
        for index, (source, target) in enumerate(zip(table_sources, table_refs))
    ]
    for load in loads:
        load.start()

    spread(count_ref, cell_ref, frac_ref, charge_ref, grid_ref)
    for load in loads[:2]:
        load.wait()
    down_ref, down_z_ref, stacked_ref = table_refs
    restrict(grid_ref, down_ref, down_z_ref, middle_ref, low_ref)
    pl.semaphore_wait(barrier, len(around))

    sources = (grid_ref, middle_ref, low_ref)
    copies = {}
    for index, message in enumerate(PLAN):
        relayed = message.relayed
        source = sources[message.source] if relayed is None else landed[PLAN.index(relayed)]
        (first, size), (low, rows) = message.local
        copies[message] = pltpu.make_async_remote_copy(
            src_ref=source.at[pl.ds(first, size), pl.ds(low, rows)],
            dst_ref=landed[index],
            send_sem=send_sem.at[index],
            recv_sem=recv_sem.at[index],
            device_id=device(*message.hop),
            device_id_type=MESH,
        )
    arrived = set()

    def arrive(message):
        if message not in arrived:
            arrived.add(message)
            copies[message].wait_recv()

    for message in FIRST:
        copies[message].start()
    loads[2].wait()
    up_ref, *parts = [Part(stacked_ref, place) for place in places]

    level_tables = [parts[6 * level : 6 * level + 6] for level in range(LEVELS)]
    for level in (2, 1, 0):
        build_taps(level, kernels[level], padded_ref, *level_tables[level][4:], reals[level], imags[level])

    for level in range(LEVELS):
        windows[level][...] = jnp.zeros_like(windows[level])
    edges_ref[...] = jnp.zeros_like(edges_ref)
    windows[0][:, :CY, :] = grid_ref[: CX + 1]
    for x in range(CX + 1):
        windows[0][x, CY : CY + 1, :] = grid_ref[CX + 1, strip_row(x) : strip_row(x) + 1, :]
    windows[1][HALF : HALF + BX[1] + 1, : ROWS[1], :] = middle_ref[...]
    windows[2][HALF : HALF + BX[2] + 1, : ROWS[2], :] = low_ref[:, : ROWS[2], :]

    for message in SECOND:
        if message.kind in ('near', 'far'):
            arrive(message.relayed)
            copies[message].start()
    def run(level, source_ref, layers, fresh):
        slots = {layer: slot for slot, layer in enumerate(layers)}
        taps = (reals[level], imags[level])
        tables = level_tables[level][:4]
        add_spectra(level, source_ref, slots, taps, tables, along_z[level], spectra[level], sums[level], fresh)

    fine = [message for message in PLAN if message.kind in ("face", "strip")]
    for message in fine:
        if message.dx == 0:
            arrive(message)
            add_fine(windows[0], message, landed[PLAN.index(message)])
    run(0, windows[0], range(HALF, HALF + CX + 1), True)
    for message in SECOND:
        if message.kind not in ('near', 'far'):
            arrive(message.relayed)
            copies[message].start()
    for message in PLAN:
        if message.kind in ("near", "far"):
            arrive(message)
            add_low(windows, message, landed[PLAN.index(message)])
    below = []
    for level in (1, 2):
        run(level, windows[level], range(BX[level] + 1 + 2 * HALF), True)
        below += from_spectra(level, level_tables[level][:4], sums[level])
    high, low = split(jnp.concatenate(below, axis=0))
    both = matmul(up_ref[...], jnp.concatenate([high, low], axis=1))
    out_ref[...] = (both[:, :LANES] + both[:, LANES:]).reshape(out_ref.shape)
    for message in PLAN:
        copies[message].wait_send()
    for message in fine:
        if message.dx != 0:
            arrive(message)
            add_fine(edges_ref, message, landed[PLAN.index(message)])
    last = CX + 1 + 2 * HALF
    run(0, edges_ref, [*range(REACH), *range(last - REACH, last)], False)
    layers = from_spectra(0, level_tables[0][:4], sums[0])
    for x in range(CX + 1):
        out_ref[x] = out_ref[x] + layers[x][:CY]
        at = slice(strip_row(x), strip_row(x) + 1)
        out_ref[CX + 1, at, :] = out_ref[CX + 1, at, :] + layers[x][CY : CY + 1]


def force_kernel(count_ref, cell_ref, frac_ref, charge_ref, grid_ref, potential_ref, forces_ref, left_ref):
    slots = cell_ref.shape[-1]
    potential_ref[...] = grid_ref[:CX]
    forces_ref[...] = jnp.zeros_like(forces_ref)
    left_ref[...] = jnp.concatenate(split(grid_ref[...].reshape(GRID_ROWS, LANES)), axis=1)
    count = jnp.max(count_ref[...].astype(jnp.float32)).astype(jnp.int32)

    def pick(values, base):
        width = CX // 2
        while width >= 1:
            bit = (base & width) != 0
            values = [jnp.where(bit, values[width + k], values[k]) for k in range(width + 1)]
            width //= 2
        return values

    def chunk(index):
        part = pl.ds(pl.multiple_of(index * FORCE_CHUNK, FORCE_CHUNK), FORCE_CHUNK)
        base_x, base_y, base_z = bases(cell_ref[0, :, part])
        row = rows_iota(16, FORCE_CHUNK)
        one, nothing = [jnp.full((16, FORCE_CHUNK), value, jnp.bfloat16) for value in (1.0, 0.0)]
        found = []
        for at_z in (base_z, (base_z + 1) & (NZ - 1)):
            target = wide(at_z, jnp.int16)
            chosen = [jnp.where((row + z).astype(jnp.int16) == target, one, nothing) for z in range(0, NZ, 16)]
            found.append(matmul(left_ref[...], jnp.concatenate(chosen * 2, axis=0)))
        shape = (8, FORCE_CHUNK)
        f = [jnp.broadcast_to(frac_ref[k, 0, :, part], shape) for k in range(3)]
        slot = index * FORCE_CHUNK + lax.broadcasted_iota(jnp.int32, (1, FORCE_CHUNK), 1)
        charge = jnp.where(slot < count, charge_ref[0, :, part], 0.0)
        base_x = jnp.broadcast_to(base_x, shape)
        base_y = jnp.broadcast_to(base_y, shape)
        row = rows_iota(*shape)
        across, along, slope = [jnp.zeros(shape, jnp.float32) for _ in range(3)]
        for tile in range(CY // 8):
            ends = []
            for values in found:
                rows = [values[x * CY + tile * 8 : x * CY + tile * 8 + 8] for x in range(CX + 1)]
                ends.append(pick(rows, base_x))
            rise = [ends[1][k] - ends[0][k] for k in range(2)]
            level = [ends[0][k] + f[2] * rise[k] for k in range(2)]
            step_x = level[1] - level[0]
            lower, upper = row + tile * 8 == base_y, row + tile * 8 == base_y + 1
            weight = jnp.where(lower, 1.0 - f[1], jnp.where(upper, f[1], 0.0))
            sign = jnp.where(lower, -1.0, jnp.where(upper, 1.0, 0.0))
            across = across + weight * step_x
            along = along + sign * (level[0] + f[0] * step_x)
            slope = slope + weight * (rise[0] + f[0] * (rise[1] - rise[0]))
        ends = []
        for values in found:
            low, high = [jnp.zeros(shape, jnp.float32) for _ in range(2)]
            for tile in range(CY // 8):
                value = values[(CX + 1) * CY + tile * 8 : (CX + 1) * CY + tile * 8 + 8]
                layer = row + (tile * 8 if tile < 2 else 12)
                if tile == 1:
                    layer = jnp.where(layer < 12, layer, -5)
                low = jnp.where(layer == base_x, value, low)
                high = jnp.where(layer == base_x + 1, value, high)
            ends.append((low, high))
        edge = base_y == CY - 1
        weight = jnp.where(edge, f[1], 0.0)
        rise = [ends[1][k] - ends[0][k] for k in range(2)]
        level = [ends[0][k] + f[2] * rise[k] for k in range(2)]
        across = across + weight * (level[1] - level[0])
        along = along + jnp.where(edge, level[0] + f[0] * (0.0 - level[0]) + f[0] * level[1], 0.0)
        slope = slope + weight * (rise[0] + f[0] * (0.0 - rise[0]) + f[0] * rise[1])
        for k, value in enumerate((across, along, slope)):
            forces_ref[k, 0, :, part] = -charge * jnp.sum(value, axis=0, keepdims=True)

    def step(index, carry):
        for k in range(FORCE_UNROLL):
            chunk(index * FORCE_UNROLL + k)
        return carry

    width = FORCE_CHUNK * FORCE_UNROLL
    lax.fori_loop(0, jnp.minimum(pl.cdiv(count, width), slots // width), step, 0)


VMEM = pl.BlockSpec(memory_space=pltpu.VMEM)
ANY = pl.BlockSpec(memory_space=pl.ANY)


def solution(mesh):
    sizes = (mesh.shape["gx"], mesh.shape["gy"])
    constants, places = tables()

    def per_device(atom_cell, atom_frac, atom_charge, atom_count, fine_kernel, middle_kernel, coarse_kernel):
        slots = atom_cell.shape[-1]
        f32 = jnp.float32
        grid = (CX + 2, CY, LANES)
        scratch = [
            pltpu.VMEM(grid, f32),
            pltpu.VMEM((BX[1] + 1, ROWS[1], LANES), f32),
            pltpu.VMEM((BX[2] + 1, ROWS[1], LANES), f32),
            pltpu.VMEM((KERNEL, 16, LANES), f32),
        ]
        scratch += [pltpu.VMEM(table.shape, jnp.dtype(table.dtype)) for table in constants]
        scratch += [pltpu.VMEM((WINDOW[k], PERIOD[k], LANES), f32) for k in range(LEVELS)]
        scratch += [pltpu.VMEM((KERNEL, PERIOD[k], LANES), f32) for k in range(LEVELS)] * 2
        scratch += [pltpu.VMEM((WINDOW[k] * PERIOD[k], 2 * LANES), f32) for k in range(LEVELS)]
        scratch += [pltpu.VMEM((SPECTRA[k], 2 * PERIOD[k], LANES), f32) for k in range(LEVELS)]
        scratch += [pltpu.VMEM((PAIR[k], 2 * PERIOD[k], LANES), f32) for k in range(LEVELS)]
        scratch += [pltpu.VMEM((2 * REACH, PERIOD[0], LANES), f32)]
        scratch += [pltpu.VMEM((message.layers[1], message.rows[1], LANES), f32) for message in PLAN]
        scratch += [pltpu.SemaphoreType.DMA((len(PLAN),))] * 2 + [pltpu.SemaphoreType.DMA((len(constants),))]
        extended = pl.pallas_call(
            lambda *refs: grid_kernel(sizes, len(constants), places, *refs),
            out_shape=pltpu.VMEM(grid, f32),
            in_specs=[VMEM] * 7 + [ANY] * len(constants),
            out_specs=VMEM,
            scratch_shapes=scratch,
            compiler_params=pltpu.CompilerParams(collective_id=0, has_side_effects=True),
            name="grid",
        )(
            atom_count,
            atom_cell,
            atom_frac,
            atom_charge,
            fine_kernel,
            middle_kernel,
            coarse_kernel,
            *[jnp.asarray(table) for table in constants],
        )
        potential, forces = pl.pallas_call(
            force_kernel,
            out_shape=(jax.ShapeDtypeStruct((CX, CY, NZ), f32), jax.ShapeDtypeStruct((3, 1, 1, slots), f32)),
            in_specs=[VMEM] * 5,
            out_specs=(VMEM, VMEM),
            scratch_shapes=[pltpu.VMEM((GRID_ROWS, 2 * LANES), jnp.bfloat16)],
            name="forces",
        )(atom_count, *[pltpu.with_memory_space_constraint(x, pltpu.VMEM) for x in (atom_cell, atom_frac, atom_charge, extended)])
        return potential, forces

    return jax.shard_map(
        per_device,
        mesh=mesh,
        in_specs=(
            P("gx", "gy", None),
            P(None, "gx", "gy", None),
            P("gx", "gy", None),
            P("gx", "gy"),
            P(),
            P(),
            P(),
        ),
        out_specs=(P("gx", "gy", None), P(None, "gx", "gy", None)),
        check_vma=False,
    )
```

profile of v0, /device:TPU:1, one launch (start us, length us, event | category | flops | bytes accessed | tf_op | source)
XLA Modules:
  0.0 20.6 jit_solution(14052153523448333023)
XLA Ops:
  0.6 0.0 copy-start.2
  0.6 0.0 copy-start
  0.7 0.0 copy-start.1
  1.3 17.2 %grid.1.grid_ref = f32[18,24,128]{2,1,0:T(8,128)S(1)} custom-call(s32[1,1]{1,0:T(1,128)S(6)} %copy.12.refs_0_.count_ref, s32[1,1,4096]{2,1,0:T(1,128)} %cell_ref.1, f32[3,1,1,4096]{3,2,1,0:T(1,128)} %frac_ref.1, f32[1,1,4096]{2,1,0:T(1,128)} %charge_ref.1, f32[9,9,9]{2,1,0:T(8,128)} %refs_4_.1, f32[9,9,9]{2,1,0:T(8,128)} %refs_5_.1, f32[9,9,9]{2,1,0:T(8,128)} %refs_6_.1, ...), custom_call_target="tpu_custom_call" | custom-call | tf_op jit(solution)/shard_map/grid/pallas_call | solution.py:729
  18.5 0.0 copy-done.2
  18.5 0.0 copy-done
  18.5 0.0 copy-done.1
  18.6 2.1 %forces.1 = (f32[16,24,128]{2,1,0:T(8,128)}, f32[3,1,1,4096]{3,2,1,0:T(1,128)}) custom-call(s32[1,1]{1,0:T(1,128)S(6)} %copy.12.refs_0_.count_ref, s32[1,1,4096]{2,1,0:T(1,128)S(1)} %copy-done.1, f32[3,1,1,4096]{3,2,1,0:T(1,128)S(1)} %copy-done, f32[1,1,4096]{2,1,0:T(1,128)S(1)} %copy-done.2, f32[18,24,128]{2,1,0:T(8,128)S(1)} %grid.1.grid_ref), custom_call_target="tpu_custom_call" | custom-call | tf_op jit(solution)/shard_map/forces/pallas_call | solution.py:747
Async XLA Ops:
  0.6 17.9 %copy-start.2 = (f32[1,1,4096]{2,1,0:T(1,128)S(1)}, f32[1,1,4096]{2,1,0:T(1,128)}, u32[]{:S(2)}) copy-start(f32[1,1,4096]{2,1,0:T(1,128)} %charge_ref.1) | copy-start | bytes 49156
  0.6 17.9 %copy-start = (f32[3,1,1,4096]{3,2,1,0:T(1,128)S(1)}, f32[3,1,1,4096]{3,2,1,0:T(1,128)}, u32[]{:S(2)}) copy-start(f32[3,1,1,4096]{3,2,1,0:T(1,128)} %frac_ref.1) | copy-start | bytes 147460
  0.7 17.9 %copy-start.1 = (s32[1,1,4096]{2,1,0:T(1,128)S(1)}, s32[1,1,4096]{2,1,0:T(1,128)}, u32[]{:S(2)}) copy-start(s32[1,1,4096]{2,1,0:T(1,128)} %cell_ref.1) | copy-start | bytes 49156
where the time goes:
time: 20.8 us; the launch traced here: 20.6 us
  Pallas kernels  19.2 us (92%)
  between operations  1.36 us (7%)
    pallas_call x1, Pallas kernels, per_device(): pl.pallas_call(lambda *refs: grid_kernel(sizes, len(constants), places, *...  17.2 us
    pallas_call x1, Pallas kernels, per_device(): pl.pallas_call(force_kernel, out_shape=(jax.ShapeDtypeStruct((CX, CY, NZ)...  2.05 us

commit v1 on v0

--- a/solution.py
+++ b/solution.py
@@ -232,7 +232,7 @@
     base_x, base_y, base_z = bases(cell_ref[0, :, part])
     f = [frac_ref[k, 0, :, part] for k in range(3)]
     slot = start + lax.broadcasted_iota(jnp.int32, (1, SPREAD_PART), 1)
-    charge = jnp.where(slot < count_ref[...], charge_ref[0, :, part], 0.0)
+    charge = jnp.where(slot < count_ref[0, 0], charge_ref[0, :, part], 0.0)
     nothing = jnp.zeros((16, SPREAD_PART), bf16)
     x_at, x_next = wide(base_x, i16), wide(base_x + 1, i16)
     y_at, y_next = wide(base_y, i16), wide(base_y + 1, i16)
@@ -627,7 +627,7 @@
     potential_ref[...] = grid_ref[:CX]
     forces_ref[...] = jnp.zeros_like(forces_ref)
     left_ref[...] = jnp.concatenate(split(grid_ref[...].reshape(GRID_ROWS, LANES)), axis=1)
-    count = jnp.max(count_ref[...].astype(jnp.float32)).astype(jnp.int32)
+    count = count_ref[0, 0]
 
     def pick(values, base):
         width = CX // 2
@@ -700,6 +700,7 @@
 
 
 VMEM = pl.BlockSpec(memory_space=pltpu.VMEM)
+SMEM = pl.BlockSpec(memory_space=pltpu.SMEM)
 ANY = pl.BlockSpec(memory_space=pl.ANY)
 
 
@@ -729,7 +730,7 @@
         extended = pl.pallas_call(
             lambda *refs: grid_kernel(sizes, len(constants), places, *refs),
             out_shape=pltpu.VMEM(grid, f32),
-            in_specs=[VMEM] * 7 + [ANY] * len(constants),
+            in_specs=[SMEM] + [VMEM] * 6 + [ANY] * len(constants),
             out_specs=VMEM,
             scratch_shapes=scratch,
             compiler_params=pltpu.CompilerParams(collective_id=0, has_side_effects=True),
@@ -747,7 +748,7 @@
         potential, forces = pl.pallas_call(
             force_kernel,
             out_shape=(jax.ShapeDtypeStruct((CX, CY, NZ), f32), jax.ShapeDtypeStruct((3, 1, 1, slots), f32)),
-            in_specs=[VMEM] * 5,
+            in_specs=[SMEM] + [VMEM] * 4,
             out_specs=(VMEM, VMEM),
             scratch_shapes=[pltpu.VMEM((GRID_ROWS, 2 * LANES), jnp.bfloat16)],
             name="forces",

time: 20.8 us -> 20.8 us (level)
  no operation moved by 1% of the time
where the time goes in v1:
time: 20.8 us; the launch traced here: 20.6 us
  Pallas kernels  19.2 us (92%)
  between operations  1.36 us (7%)
    pallas_call x1, Pallas kernels, per_device(): pl.pallas_call(lambda *refs: grid_kernel(sizes, len(constants), places, *...  17.2 us
    pallas_call x1, Pallas kernels, per_device(): pl.pallas_call(force_kernel, out_shape=(jax.ShapeDtypeStruct((CX, CY, NZ)...  1.98 us

profile of v1, /device:TPU:1, one launch (start us, length us, event | category | flops | bytes accessed | tf_op | source)
XLA Modules:
  0.0 20.6 jit_solution(13649939525428553991)
XLA Ops:
  0.6 0.0 copy-start.2
  0.6 0.0 copy-start
  0.7 0.0 copy-start.1
  1.3 17.2 %grid.1.grid_ref = f32[18,24,128]{2,1,0:T(8,128)S(1)} custom-call(s32[1,1]{1,0:T(1,128)S(6)} %copy.12.refs_0_.count_ref, s32[1,1,4096]{2,1,0:T(1,128)} %cell_ref.1, f32[3,1,1,4096]{3,2,1,0:T(1,128)} %frac_ref.1, f32[1,1,4096]{2,1,0:T(1,128)} %charge_ref.1, f32[9,9,9]{2,1,0:T(8,128)} %refs_4_.1, f32[9,9,9]{2,1,0:T(8,128)} %refs_5_.1, f32[9,9,9]{2,1,0:T(8,128)} %refs_6_.1, ...), custom_call_target="tpu_custom_call" | custom-call | tf_op jit(solution)/shard_map/grid/pallas_call | solution.py:730
  18.6 0.0 copy-done.2
  18.6 0.0 copy-done
  18.6 0.0 copy-done.1
  18.6 2.0 %forces.1 = (f32[16,24,128]{2,1,0:T(8,128)}, f32[3,1,1,4096]{3,2,1,0:T(1,128)}) custom-call(s32[1,1]{1,0:T(1,128)S(6)} %copy.12.refs_0_.count_ref, s32[1,1,4096]{2,1,0:T(1,128)S(1)} %copy-done.1, f32[3,1,1,4096]{3,2,1,0:T(1,128)S(1)} %copy-done, f32[1,1,4096]{2,1,0:T(1,128)S(1)} %copy-done.2, f32[18,24,128]{2,1,0:T(8,128)S(1)} %grid.1.grid_ref), custom_call_target="tpu_custom_call" | custom-call | tf_op jit(solution)/shard_map/forces/pallas_call | solution.py:748
Async XLA Ops:
  0.6 17.9 %copy-start.2 = (f32[1,1,4096]{2,1,0:T(1,128)S(1)}, f32[1,1,4096]{2,1,0:T(1,128)}, u32[]{:S(2)}) copy-start(f32[1,1,4096]{2,1,0:T(1,128)} %charge_ref.1) | copy-start | bytes 49156
  0.6 17.9 %copy-start = (f32[3,1,1,4096]{3,2,1,0:T(1,128)S(1)}, f32[3,1,1,4096]{3,2,1,0:T(1,128)}, u32[]{:S(2)}) copy-start(f32[3,1,1,4096]{3,2,1,0:T(1,128)} %frac_ref.1) | copy-start | bytes 147460
  0.7 17.9 %copy-start.1 = (s32[1,1,4096]{2,1,0:T(1,128)S(1)}, s32[1,1,4096]{2,1,0:T(1,128)}, u32[]{:S(2)}) copy-start(s32[1,1,4096]{2,1,0:T(1,128)} %cell_ref.1) | copy-start | bytes 49156
